TPU v7x, 32 devices: a whole 2x2x4 slice. The times are simulated.
32 devices in a mesh: row: 8 (over z, y), col: 4 (over x, core).
Axes of the slice: x: 2, y: 2, z: 4, core: 2. Of those that a mesh axis runs over, the one named last changes fastest.
Arguments:
- tensor: bfloat16 [2048, 8192], P(('row', 'col')), may hold values from -6 to 6
- density: bfloat16 [2, 4096, 8192], P(None, 'col', 'row'), may hold values from -0.125 to 0.125
- tensor_mask: int32 [16, 64], replicated, may hold values 0 or 1
- density_mask: int32 [64, 64], replicated, may hold values 0 or 1
- pair_rows: int32 [32], replicated, may hold values from 0 to 31, as said below
Outputs:
- contracted: bfloat16 [2048, 8192], P(('row', 'col'))
Inputs may be any that keep to these rules, and one draw needn't show every extreme that they name: pair_rows is a permutation of 0 to 31. Among the 8 slots that share one remainder modulo 4, at most 3 hold units of any one group of 8 consecutive units, and for every remainder some group gets exactly 3.
All inputs are finite; a program needn't handle non-finite values.
Results may differ from a plain program's by a relative error of at most 0.001.
Values may be sent and summed in bfloat16 or wider, within the bound.
A program may use at most 64 MiB of HBM per device.

v0:
```python
import jax
import jax.numpy as jnp
from jax import lax
from jax.sharding import PartitionSpec as P

BLOCK = 128


def on_device(tensor, density, tensor_mask, density_mask, pair_rows):
    row_count = lax.axis_size("row")
    col_count = lax.axis_size("col")
    row_index = lax.axis_index("row")
    col_index = lax.axis_index("col")
    unit_rows, orbitals = tensor.shape
    owner_slot = row_index * col_count + col_index
    own_unit = pair_rows[owner_slot]
    mask_rows = (own_unit * unit_rows + jnp.arange(unit_rows, dtype=jnp.int32)) // BLOCK
    row_mask = jnp.repeat(
        jnp.take(tensor_mask, mask_rows, axis=0).astype(jnp.bfloat16), BLOCK, axis=1
    )
    masked = tensor * row_mask
    piece_rows = density.shape[1]
    piece_width = density.shape[2]
    half_rows = orbitals // 2
    global_rows = (
        jnp.arange(2)[:, None] * half_rows
        + col_index * piece_rows
        + jnp.arange(piece_rows)[None, :]
    )
    global_cols = row_index * piece_width + jnp.arange(piece_width)
    dens_mask = jnp.take(
        jnp.take(density_mask, (global_rows // BLOCK).reshape(-1), axis=0),
        global_cols // BLOCK,
        axis=1,
    )
    density_pair = density * dens_mask.reshape(2, piece_rows, piece_width).astype(jnp.bfloat16)
    column = lax.all_gather(density_pair, "col", axis=1, tiled=True).reshape(orbitals, piece_width)
    tile_result = jnp.dot(
        lax.all_gather(masked, "row", axis=0, tiled=True),
        column,
        preferred_element_type=jnp.float32,
    ).astype(jnp.bfloat16)
    tile_result = tile_result.reshape(row_count, unit_rows, piece_width)
    owned_rows = lax.all_to_all(tile_result, "row", split_axis=0, concat_axis=2, tiled=True)
    return owned_rows.reshape(unit_rows, orbitals)


def solution(mesh):
    placed = (P(("row", "col"), None), P(None, "col", "row"), P(), P(), P())
    return jax.shard_map(
        on_device, mesh=mesh, in_specs=placed, out_specs=P(("row", "col"), None), check_vma=False
    )
```

profile of v0, /device:TPU:0, one launch (start us, length us, event | category | flops | bytes accessed | tf_op | source)
XLA Modules:
  0.0 300.5 jit_solution(1032798503816356706)
XLA Ops:
  6.5 0.0 copy-start
  6.5 0.0 all-gather.3.cloned.1.call-start
  6.5 1.2 dynamic_slice.3
  8.5 1.3 gather_fusion
  9.8 0.1 select_convert_fusion.1
  9.9 0.6 broadcast_in_dim.37
  10.5 2.9 bitcast_multiply_fusion
  13.4 0.0 all-gather.3.cloned.1.call-update
  13.4 0.0 all-gather.5.cloned.1.call-start
  13.5 0.1 fusion.4
  13.6 0.0 copy-done
  13.6 5.5 %gather_fusion.1 = s32[2048,64]{1,0:T(8,128)S(1)} fusion(s32[64,64]{1,0:T(8,128)S(1)} %copy-done, s32[2048]{0:T(1024)S(1)} %broadcast_clamp_fusion), kind=kCustom, calls=%fused_computation.1 | custom fusion | bytes 1056768 | tf_op jit(solution)/shard_map/jit(_take)/gather | solution.py:32
  19.1 0.3 broadcast_select_fusion
  19.5 0.3 copy.9
  19.8 6.8 %gather_fusion.2 = s32[1024,2048]{1,0:T(8,128)} fusion(s32[2048,64]{0,1:T(8,128)S(1)} %copy.9, s32[1024]{0:T(1024)S(1)} %broadcast_clamp_fusion.1), kind=kCustom, calls=%fused_computation.2 | custom fusion | bytes 16781312 | tf_op jit(solution)/shard_map/jit(_take)/gather | solution.py:31
  26.7 9.3 %copy.12 = s32[2048,1024]{1,0:T(8,128)} copy(s32[2048,1024]{0,1:T(8,128)} %bitcast.47) | data formatting | bytes 16777216 | tf_op jit(solution)/shard_map/jit(_take)/gather | solution.py:31
  36.0 8.3 %fusion = bf16[2,1024,1024]{2,1,0:T(8,128)(2,1)} fusion(bf16[2,1024,1024]{2,1,0:T(8,128)(2,1)} %param.6, s32[2,1024,1024]{2,1,0:T(8,128)} %bitcast.48, pred[1024]{0:T(1024)(128)(4,1)S(1)} %compare_and_fusion.1), kind=kLoop, calls=%fused_computation.4 | loop fusion | flops 6291456 | bytes 16778240 | tf_op jit(solution)/shard_map/mul | solution.py:36
  44.3 0.0 all-gather.5.cloned.1.call-update
  44.3 96.4 %all-gather.3.cloned.1.call-done = bf16[512,8192]{1,0:T(8,128)(2,1)} async-done(((bf16[64,8192]{1,0:T(8,128)(2,1)}), bf16[512,8192]{1,0:T(8,128)(2,1)}) %all-gather.3.cloned.1.call-update) | async-done | bytes 8388624 | tf_op jit(solution)/shard_map/all_gather | solution.py:39
  140.7 105.7 %all-gather.5.cloned.1.call-done = bf16[2,4096,1024]{2,1,0:T(8,128)(2,1)} async-done(((bf16[2,1024,1024]{2,1,0:T(8,128)(2,1)}), bf16[2,4096,1024]{2,1,0:T(8,128)(2,1)}) %all-gather.5.cloned.1.call-update) | async-done | bytes 16777232 | tf_op jit(solution)/shard_map/all_gather | solution.py:37
  246.4 14.8 %convolution_convert_fusion = bf16[512,1024]{1,0:T(8,128)(2,1)S(1)} fusion(bf16[512,8192]{1,0:T(8,128)(2,1)} %all-gather.3.cloned.1.call-done, bf16[8192,1024]{1,0:T(8,128)(2,1)} %bitcast.55), kind=kOutput, calls=%fused_computation.5 | convolution fusion | flops 8590458880 | bytes 26214400 | tf_op jit(solution)/shard_map/dot_general | solution.py:38
  261.2 31.5 %all_to_all.15 = bf16[8,64,1024]{2,1,0:T(8,128)(2,1)S(1)} all-to-all(bf16[8,64,1024]{2,1,0:T(8,128)(2,1)S(1)} %bitcast.51), channel_id=1, replica_groups=mesh['row'=8,'col'=4] {'row'}, dimensions={0} | all-to-all | bytes 2097152 | tf_op jit(solution)/shard_map/all_to_all | solution.py:44
  292.6 1.1 copy.16
  (11 shorter events, 0.2 us)
Async XLA Ops:
  6.5 7.1 %copy-start = (s32[64,64]{1,0:T(8,128)S(1)}, s32[64,64]{1,0:T(8,128)}, u32[]{:S(2)}) copy-start(s32[64,64]{1,0:T(8,128)} %param.8) | copy-start | bytes 49156
  6.5 134.2 %all-gather.3.cloned.1.call-start = ((), (), s32[]{:S(2)}) async-start(), calls=%async_computation.1 | async-start | bytes 9437184 | tf_op jit(solution)/shard_map/all_gather | solution.py:39
  13.4 233.0 %all-gather.5.cloned.1.call-start = ((), (), s32[]{:S(2)}) async-start(), calls=%async_computation.2 | async-start | bytes 20971520 | tf_op jit(solution)/shard_map/all_gather | solution.py:37
Sparse Core Ops, SparseCore 0:
  13.5 127.1 all-gather.2
  142.3 104.0 all-gather.4
where the time goes:
time: 301 us
  waiting for transfers between devices  202 us (67%)
  blocking collectives  31.5 us (10%)
  local copies, waits for them, and re-layouts  26.1 us (9%)
  matrix products  14.8 us (5%)
  between operations  14.2 us (5%)
  other arithmetic  11.8 us (4%)
    all_gather x1, waiting for transfers between devices, on_device(): lax.all_gather(density_pair, 'col', axis=1, tiled=True)  106 us
    all_gather x1, waiting for transfers between devices, on_device(): lax.all_gather(masked, 'row', axis=0, tiled=True)  96.4 us
    all_to_all x1, blocking collectives, on_device(): lax.all_to_all(tile_result, 'row', split_axis=0, concat_axis=2, tiled=True)  31.5 us
    gather x2, local copies, waits for them, and re-layouts, on_device(): jnp.take(jnp.take(density_mask, (global_rows // BLOCK).reshape(-1), axis=...  16.1 us
    dot_general x1, matrix products, on_device(): jnp.dot(lax.all_gather(masked, 'row', axis=0, tiled=True), column, prefer...  14.8 us
    mul x1, other arithmetic, on_device(): density * dens_mask.reshape(2, piece_rows, piece_width).astype(jnp.bfloat16)  8.29 us
  transfers between devices with their start and end apart: 2, of which 2 were waited for; matrix products, arithmetic and copies ran while one was open for 10% of the time, Pallas kernels for 0%

commit v1 on v0

v1 whole, which is shorter than its diff:
```python
import functools

import jax
import jax.numpy as jnp
from jax import lax
from jax.experimental import pallas as pl
from jax.experimental.pallas import tpu as pltpu
from jax.sharding import PartitionSpec as P

BLOCK = 128
CORES = 2
MESH = pl.DeviceIdType.MESH


def kernel(
    dims, t_ref, d_ref, tm_ref, dm_ref, pr_ref, out_ref,
    a_raw, a_m, b_raw, b_m, acc, res,
    a_recv, a_send, b_recv, b_send, o_recv, o_send, loc,
):
    n_row, n_col, hi_n, lo_n, x_n, chunks = dims
    r = lax.axis_index("row")
    c = lax.axis_index("col")
    hi, lo = r // lo_n, r % lo_n
    x, core = c // CORES, c % CORES
    rows, orbitals = t_ref.shape
    piece_rows, width = d_ref.shape[1], d_ref.shape[2]
    half = orbitals // 2
    w = width // chunks
    late = []

    def when_static(cond, body):
        if cond is True:
            body()
        else:
            pl.when(cond)(body)

    barrier = pltpu.get_barrier_semaphore()

    def greet(peer):
        pl.semaphore_signal(barrier, inc=1, device_id=peer, device_id_type=MESH)

    for q in range(1, n_row):
        greet(((r + q) % n_row, c))
    greet((r, x * CORES + (core + 1) % CORES))
    pl.when(x > 0)(lambda: greet((r, c - CORES)))
    pl.when(x < x_n - 1)(lambda: greet((r, c + CORES)))
    expected = n_row + (x > 0).astype(jnp.int32) + (x < x_n - 1).astype(jnp.int32)
    pl.semaphore_wait(barrier, expected)

    def row_of(h, l):
        return h * lo_n + l

    def slot_of(h, l):
        return l * hi_n + h

    def a_copy(way, h, l, dest, own=False):
        s = slot_of(h, l)
        return pltpu.make_async_remote_copy(
            src_ref=t_ref if own else a_raw.at[s],
            dst_ref=a_raw.at[s],
            send_sem=a_send.at[way, s],
            recv_sem=a_recv.at[s],
            device_id=(dest, c),
            device_id_type=MESH,
        )

    def a_go(cond, way, h, l, dest, own=False):
        when_static(cond, lambda: a_copy(way, h, l, dest, own).start())
        late.append((cond, lambda: a_copy(way, h, l, dest, own).wait_send()))

    def a_wait(h, l):
        a_copy(0, h, l, r).wait_recv()

    def a_lo_go(cond, h, own=False):
        left = lo > 0
        right = lo < lo_n - 1
        a_go(jnp.logical_and(cond, left), 2, h, lo, r - 1, own)
        a_go(jnp.logical_and(cond, right), 3, h, lo, r + 1, own)

    def b_copy(way, j, cc, dest, own=False):
        return pltpu.make_async_remote_copy(
            src_ref=d_ref.at[:, :, pl.ds(j * w, w)] if own else b_raw.at[cc, j],
            dst_ref=b_raw.at[cc, j],
            send_sem=b_send.at[way, cc, j],
            recv_sem=b_recv.at[cc, j],
            device_id=(r, dest),
            device_id_type=MESH,
        )

    def b_go(cond, way, j, cc, dest, own=False):
        when_static(cond, lambda: b_copy(way, j, cc, dest, own).start())
        late.append((cond, lambda: b_copy(way, j, cc, dest, own).wait_send()))

    def b_wait(j, cc):
        b_copy(0, j, cc, c).wait_recv()

    other = x * CORES + (core + 1) % CORES
    own_slot = slot_of(hi, lo)
    true = hi >= 0

    a_go(hi > 0, 0, hi, lo, row_of(hi - 1, lo), own=True)
    a_go(hi < hi_n - 1, 1, hi, lo, row_of(hi + 1, lo), own=True)
    a_lo_go(true, hi, own=True)
    for j in range(chunks):
        b_go(x > 0, 0, j, c, c - CORES, own=True)
        b_go(x < x_n - 1, 1, j, c, c + CORES, own=True)
    own_a = pltpu.make_async_copy(t_ref, a_raw.at[own_slot], loc.at[chunks])
    own_a.start()
    own_b = [
        pltpu.make_async_copy(d_ref.at[:, :, pl.ds(j * w, w)], b_raw.at[c, j], loc.at[j])
        for j in range(chunks)
    ]
    for j in range(chunks):
        own_b[j].start()
        b_go(True, 2, j, c, other, own=True)

    def mask_a(h, l):
        s = slot_of(h, l)
        unit = pr_ref[row_of(h, l) * n_col + c]
        mask_row = (unit * rows) // BLOCK

        def body(jb, _):
            m = tm_ref[mask_row, jb].astype(jnp.float32)
            mv = jnp.full((16, BLOCK), m, jnp.float32).astype(jnp.bfloat16)
            cols = pl.ds(pl.multiple_of(jb * BLOCK, BLOCK), BLOCK)
            v = a_raw[s, :, cols].reshape(rows // 16, 16, BLOCK) * mv[None]
            a_m[l, pl.ds(pl.multiple_of(h * rows, rows), rows), cols] = v.reshape(rows, BLOCK)
            return 0

        lax.fori_loop(0, orbitals // BLOCK, body, 0)

    blocks_k = piece_rows // BLOCK

    def mask_b(j):
        def body(i, _):
            kb = i % blocks_k
            ch = i // blocks_k
            cc, h = ch // 2, ch % 2
            src = pl.ds(pl.multiple_of(kb * BLOCK, BLOCK), BLOCK)
            k = h * half + cc * piece_rows + kb * BLOCK
            dst = pl.ds(pl.multiple_of(k, BLOCK), BLOCK)
            for jb in range(w // BLOCK):
                m = dm_ref[k // BLOCK, (r * width + j * w) // BLOCK + jb].astype(jnp.float32)
                mv = jnp.full((16, BLOCK), m, jnp.float32).astype(jnp.bfloat16)
                cols = pl.ds(jb * BLOCK, BLOCK)
                v = b_raw[cc, j, h, src, cols].reshape(BLOCK // 16, 16, BLOCK) * mv[None]
                b_m[j, dst, cols] = v.reshape(BLOCK, BLOCK)
            return 0

        lax.fori_loop(0, n_col * 2 * blocks_k, body, 0)

    kc = orbitals // 4

    def o_copy(q, h, j, dest, sender):
        return pltpu.make_async_remote_copy(
            src_ref=res.at[q, j, pl.ds(h * rows, rows)],
            dst_ref=out_ref.at[:, pl.ds(pl.multiple_of(sender * width + j * w, BLOCK), w)],
            send_sem=o_send.at[q, h, j],
            recv_sem=o_recv.at[sender, j],
            device_id=(dest, c),
            device_id_type=MESH,
        )

    def o_local(h, j):
        return pltpu.make_async_copy(
            res.at[0, j, pl.ds(h * rows, rows)],
            out_ref.at[:, pl.ds(pl.multiple_of(r * width + j * w, BLOCK), w)],
            o_send.at[0, h, j],
        )

    def unit(q, j):
        g = (lo + q) % lo_n
        acc[...] = jnp.zeros_like(acc)

        def body(k, _):
            ks = pl.ds(pl.multiple_of(k * kc, kc), kc)
            acc[...] += jnp.dot(a_m[g, :, ks], b_m[j, ks, :], preferred_element_type=jnp.float32)
            return 0

        lax.fori_loop(0, orbitals // kc, body, 0)
        res[q, j] = acc[...].astype(jnp.bfloat16)
        for h in range(hi_n):
            dest = row_of(h, g)
            if q == 0:
                pl.when(hi != h)(lambda: o_copy(q, h, j, dest, r).start())
                pl.when(hi == h)(lambda: o_local(h, j).start())
                late.append((hi != h, functools.partial(
                    lambda q, h, j, dest: o_copy(q, h, j, dest, r).wait_send(), q, h, j, dest)))
                late.append((hi == h, functools.partial(lambda h, j: o_local(h, j).wait(), h, j)))
            else:
                o_copy(q, h, j, dest, r).start()
                late.append((True, functools.partial(
                    lambda q, h, j, dest: o_copy(q, h, j, dest, r).wait_send(), q, h, j, dest)))

    def b_arrive(j):
        for e in range(1, x_n):
            for sign in (-1, 1):
                xx = x + sign * e
                there = jnp.logical_and(xx >= 0, xx < x_n)
                cc = xx * CORES + core
                pl.when(there)(lambda: b_wait(j, cc))
                onward = x - sign
                more = jnp.logical_and(there, jnp.logical_and(onward >= 0, onward < x_n))
                b_go(more, 0 if sign > 0 else 1, j, cc, onward * CORES + core)
                b_go(there, 2, j, cc, other)

    def b_finish(j):
        own_b[j].wait()
        for xx in range(x_n):
            b_wait(j, xx * CORES + (core + 1) % CORES)
        mask_b(j)

    def line_arrive(d):
        for sign in (-1, 1):
            h = hi + sign * d
            there = jnp.logical_and(h >= 0, h < hi_n)
            pl.when(there)(lambda: a_wait(h, lo))
            onward = hi - sign
            more = jnp.logical_and(there, jnp.logical_and(onward >= 0, onward < hi_n))
            a_go(more, 0 if sign > 0 else 1, h, lo, row_of(onward, lo))
            a_lo_go(there, h)

    def at_distance(d):
        if d == 0:
            return [(hi, true)]
        out = []
        for sign in (-1, 1):
            h = hi + sign * d
            out.append((h, jnp.logical_and(h >= 0, h < hi_n)))
        return out

    def lo_arrive(d):
        for h, there in at_distance(d):
            for e in range(1, lo_n):
                for sign in (-1, 1):
                    l = lo + sign * e
                    ok = jnp.logical_and(there, jnp.logical_and(l >= 0, l < lo_n))
                    pl.when(ok)(lambda: a_wait(h, l))
                    onward = lo - sign
                    more = jnp.logical_and(ok, jnp.logical_and(onward >= 0, onward < lo_n))
                    a_go(more, 2 if sign > 0 else 3, h, l, row_of(hi, onward))

    def mask_lo(d):
        for h, there in at_distance(d):
            for q in range(1, lo_n):
                g = (lo + q) % lo_n
                pl.when(there)(lambda: mask_a(h, g))

    def mask_line(d):
        for h, there in at_distance(d):
            pl.when(there)(lambda: mask_a(h, lo))

    own_a.wait()
    mask_line(0)
    for d in range(1, hi_n):
        line_arrive(d)
        b_arrive(d - 1)
        lo_arrive(d - 1)
        mask_line(d)
        mask_lo(d - 1)
        b_finish(d - 1)
    for j in range(hi_n - 1):
        unit(0, j)
    for j in range(hi_n - 1, chunks):
        b_arrive(j)
    lo_arrive(hi_n - 1)
    mask_lo(hi_n - 1)
    for j in range(hi_n - 1):
        for q in range(1, lo_n):
            unit(q, j)
    for j in range(hi_n - 1, chunks):
        b_finish(j)
        for q in range(lo_n):
            unit(q, j)

    for q in range(1, n_row):
        sender = (r + q) % n_row
        for j in range(chunks):
            o_copy(0, 0, j, r, sender).wait_recv()
    for cond, wait in late:
        when_static(cond, wait)


def on_device(dims, tensor, density, tensor_mask, density_mask, pair_rows):
    n_row, n_col, hi_n, lo_n, x_n, chunks = dims
    rows, orbitals = tensor.shape
    _, piece_rows, width = density.shape
    w = width // chunks
    bf16 = jnp.bfloat16
    any_spec = pl.BlockSpec(memory_space=pl.ANY)
    smem = pl.BlockSpec(memory_space=pltpu.SMEM)
    return pl.pallas_call(
        functools.partial(kernel, dims),
        out_shape=jax.ShapeDtypeStruct((rows, orbitals), bf16),
        in_specs=[any_spec, any_spec, smem, smem, smem],
        out_specs=any_spec,
        scratch_shapes=[
            pltpu.VMEM((n_row, rows, orbitals), bf16),
            pltpu.VMEM((lo_n, hi_n * rows, orbitals), bf16),
            pltpu.VMEM((n_col, chunks, 2, piece_rows, w), bf16),
            pltpu.VMEM((chunks, orbitals, w), bf16),
            pltpu.VMEM((hi_n * rows, w), jnp.float32),
            pltpu.VMEM((lo_n, chunks, hi_n * rows, w), bf16),
            pltpu.SemaphoreType.DMA((n_row,)),
            pltpu.SemaphoreType.DMA((4, n_row)),
            pltpu.SemaphoreType.DMA((n_col, chunks)),
            pltpu.SemaphoreType.DMA((3, n_col, chunks)),
            pltpu.SemaphoreType.DMA((n_row, chunks)),
            pltpu.SemaphoreType.DMA((lo_n, hi_n, chunks)),
            pltpu.SemaphoreType.DMA((chunks + 1,)),
        ],
        compiler_params=pltpu.CompilerParams(
            collective_id=0, has_side_effects=True, vmem_limit_bytes=60 << 20
        ),
    )(tensor, density, tensor_mask, density_mask, pair_rows)


def solution(mesh):
    n_row, n_col = mesh.shape["row"], mesh.shape["col"]
    hi_n = 1
    while hi_n * hi_n < n_row:
        hi_n *= 2
    dims = (n_row, n_col, hi_n, n_row // hi_n, n_col // CORES, max(4, hi_n))
    placed = (P(("row", "col"), None), P(None, "col", "row"), P(), P(), P())
    return jax.shard_map(
        functools.partial(on_device, dims),
        mesh=mesh,
        in_specs=placed,
        out_specs=P(("row", "col"), None),
        check_vma=False,
    )
```

time: 301 us -> 128 us (0.43)
  waiting for transfers between devices: 202 us -> 0 us
  Pallas kernels: 0 us -> 126 us
  blocking collectives: 31.5 us -> 0 us
  local copies, waits for them, and re-layouts: 26.1 us -> 2.26 us
  matrix products: 14.8 us -> 0 us
  between operations: 14.2 us -> 0.01 us
  other arithmetic: 11.8 us -> 0 us
    all_gather x2 -> x0, waiting for transfers between devices: 202 us -> none  [the longest x1 106 us: on_device(): lax.all_gather(density_pair, 'col', axis=1, tiled=True)]
    pallas_call x0 -> x1, Pallas kernels: none -> 126 us  [on_device(): pl.pallas_call(functools.partial(kernel, dims), out_shape=jax.ShapeDtypeS...]
    all_to_all x1 -> x0, blocking collectives: 31.5 us -> none  [on_device(): lax.all_to_all(tile_result, 'row', split_axis=0, concat_axis=2, tiled=True)]
    gather x4 -> x0, local copies, waits for them, and re-layouts: 22.9 us -> none  [the longest x2 16.1 us: on_device(): jnp.take(jnp.take(density_mask, (global_rows // BLOCK).reshape(-1), axis=...]
    dot_general x1 -> x0, matrix products: 14.8 us -> none  [on_device(): jnp.dot(lax.all_gather(masked, 'row', axis=0, tiled=True), column, prefer...]
    mul x2 -> x0, other arithmetic: 11.2 us -> none  [the longest x1 8.29 us: on_device(): density * dens_mask.reshape(2, piece_rows, piece_width).astype(jnp.bfloat16)]
  transfers between devices with their start and end apart: 2 -> 0, of which waited for: 2 -> 0; matrix products, arithmetic and copies ran while one was open for 10% -> 0% of each run, Pallas kernels for 0% -> 0%
where the time goes in v1:
time: 128 us
  Pallas kernels  126 us (98%)
  local copies, waits for them, and re-layouts  2.26 us (2%)
    pallas_call x1, Pallas kernels, on_device(): pl.pallas_call(functools.partial(kernel, dims), out_shape=jax.ShapeDtypeS...  126 us

profile of v1, /device:TPU:0, one launch (start us, length us, event | category | flops | bytes accessed | tf_op | source)
XLA Modules:
  0.0 128.1 jit_solution(4761894712428049582)
XLA Ops:
  0.0 125.8 %shard_map.55 = bf16[64,8192]{1,0:T(8,128)(2,1)} custom-call(bf16[64,8192]{1,0:T(8,128)(2,1)} %t_ref.1, bf16[2,1024,1024]{2,1,0:T(8,128)(2,1)} %d_ref.1, s32[16,64]{1,0:T(8,128)} %tm_ref.1, s32[64,64]{1,0:T(8,128)} %dm_ref.1, s32[32]{0:T(128)} %pr_ref.1), custom_call_target="tpu_custom_call" | custom-call | tf_op jit(solution)/shard_map/pallas_call | solution.py:292
  125.8 2.3 %copy.7 = bf16[64,8192]{1,0:T(8,128)(2,1)} copy(bf16[64,8192]{1,0:T(8,128)(2,1)} %shard_map.55) | data formatting | bytes 2097152

commit v2 on v1

v2 whole, which is shorter than its diff:
```python
import functools
import math

import jax
import jax.numpy as jnp
from jax import lax
from jax.experimental import pallas as pl
from jax.experimental.pallas import tpu as pltpu
from jax.sharding import PartitionSpec as P

BLOCK = 128
CORES = 2
MESH = pl.DeviceIdType.MESH


def kernel(
    dims, room, pa_ref, pb_ref, tm_ref, dm_ref, pr_ref, out_ref,
    a_raw, a_m, b_raw, b_m, acc, res,
    a_recv, a_send, b_recv, b_send, o_recv, o_send, loc, *stage,
):
    n_row, n_col, hi_n, lo_n, x_n, chunks = dims
    a_room, b_room = room
    piece = b_room // chunks
    a_stage, b_stage, staged = stage if stage else (None, None, None)
    r = lax.axis_index("row")
    c = lax.axis_index("col")
    hi, lo = r // lo_n, r % lo_n
    x, core = c // CORES, c % CORES
    rows = pa_ref.shape[1]
    orbitals = out_ref.shape[1]
    piece_rows, width = orbitals // 2 // n_col, orbitals // n_row
    half = orbitals // 2
    w = width // chunks
    late = []

    def when_static(cond, body):
        if cond is True:
            body()
        else:
            pl.when(cond)(body)

    barrier = pltpu.get_barrier_semaphore()

    def greet(peer):
        pl.semaphore_signal(barrier, inc=1, device_id=peer, device_id_type=MESH)

    for q in range(1, n_row):
        greet(((r + q) % n_row, c))
    greet((r, x * CORES + (core + 1) % CORES))
    pl.when(x > 0)(lambda: greet((r, c - CORES)))
    pl.when(x < x_n - 1)(lambda: greet((r, c + CORES)))
    expected = n_row + (x > 0).astype(jnp.int32) + (x < x_n - 1).astype(jnp.int32)
    pl.semaphore_wait(barrier, expected)

    def row_of(h, l):
        return h * lo_n + l

    def slot_of(h, l):
        return l * hi_n + h

    def a_copy(way, h, l, dest, own=False):
        s = slot_of(h, l)
        return pltpu.make_async_remote_copy(
            src_ref=pa_ref if own else a_raw.at[s],
            dst_ref=a_raw.at[s],
            send_sem=a_send.at[way, s],
            recv_sem=a_recv.at[s],
            device_id=(dest, c),
            device_id_type=MESH,
        )

    def a_go(cond, way, h, l, dest, own=False):
        when_static(cond, lambda: a_copy(way, h, l, dest, own).start())
        late.append((cond, lambda: a_copy(way, h, l, dest, own).wait_send()))

    def a_wait(h, l):
        a_copy(0, h, l, r).wait_recv()

    def a_lo_go(cond, h, own=False):
        left = lo > 0
        right = lo < lo_n - 1
        a_go(jnp.logical_and(cond, left), 2, h, lo, r - 1, own)
        a_go(jnp.logical_and(cond, right), 3, h, lo, r + 1, own)

    def b_part(p):
        return pl.ds(p * piece, piece)

    def b_copy(way, p, cc, dest, own=False):
        return pltpu.make_async_remote_copy(
            src_ref=pb_ref.at[b_part(p)] if own else b_raw.at[cc, b_part(p)],
            dst_ref=b_raw.at[cc, b_part(p)],
            send_sem=b_send.at[way, cc, p],
            recv_sem=b_recv.at[cc, p],
            device_id=(r, dest),
            device_id_type=MESH,
        )

    def b_go(cond, way, j, cc, dest, own=False):
        when_static(cond, lambda: b_copy(way, j, cc, dest, own).start())
        late.append((cond, lambda: b_copy(way, j, cc, dest, own).wait_send()))

    def b_wait(j, cc):
        b_copy(0, j, cc, c).wait_recv()

    other = x * CORES + (core + 1) % CORES
    own_slot = slot_of(hi, lo)
    true = hi >= 0

    a_go(hi > 0, 0, hi, lo, row_of(hi - 1, lo), own=True)
    a_go(hi < hi_n - 1, 1, hi, lo, row_of(hi + 1, lo), own=True)
    a_lo_go(true, hi, own=True)
    for j in range(chunks):
        b_go(x > 0, 0, j, c, c - CORES, own=True)
        b_go(x < x_n - 1, 1, j, c, c + CORES, own=True)
    own_a = pltpu.make_async_copy(pa_ref, a_raw.at[own_slot], loc.at[chunks])
    own_a.start()
    own_b = [
        pltpu.make_async_copy(
            pb_ref.at[b_part(j)], (b_stage if stage else b_raw).at[c, b_part(j)], loc.at[j])
        for j in range(chunks)
    ]
    for j in range(chunks):
        own_b[j].start()
        b_go(True, 2, j, c, other, own=True)

    def mask_vector(m):
        return jnp.full((16, BLOCK), m.astype(jnp.float32), jnp.float32).astype(jnp.bfloat16)

    def mask_a(h, l):
        s = slot_of(h, l)
        unit = pr_ref[row_of(h, l) * n_col + c]
        mask_row = (unit * rows) // BLOCK

        if stage:
            move = pltpu.make_async_copy(a_raw.at[s], a_stage, staged.at[n_col])
            move.start()
            move.wait()

        def body(jb, count):
            m = tm_ref[mask_row, jb]
            if stage:
                v = a_stage[jnp.minimum(count, a_room - 1)]
            else:
                v = a_raw[s, jb]
            v = v.reshape(rows // 16, 16, BLOCK)
            cols = pl.ds(pl.multiple_of(jb * BLOCK, BLOCK), BLOCK)
            to = pl.ds(pl.multiple_of(h * rows, rows), rows)
            a_m[l, to, cols] = (v * mask_vector(m)[None]).reshape(rows, BLOCK)
            return count + m

        lax.fori_loop(0, orbitals // BLOCK, body, jnp.int32(0))

    blocks_k = piece_rows // BLOCK
    seen = [jnp.int32(0)] * n_col

    def mask_b(j):
        for cc in range(n_col):
            def body(i, count):
                h, kb = i // blocks_k, i % blocks_k
                k = h * half + cc * piece_rows + kb * BLOCK
                to = pl.ds(pl.multiple_of(k, BLOCK), BLOCK)
                for jb in range(w // BLOCK):
                    m = dm_ref[k // BLOCK, (r * width + j * w) // BLOCK + jb]
                    if stage:
                        v = b_stage[cc, jnp.minimum(count, b_room - 1)]
                    else:
                        v = b_raw[cc, (j * 2 * blocks_k + i) * (w // BLOCK) + jb]
                    v = v.reshape(BLOCK // 16, 16, BLOCK)
                    cols = pl.ds(jb * BLOCK, BLOCK)
                    b_m[j, to, cols] = (v * mask_vector(m)[None]).reshape(BLOCK, BLOCK)
                    count = count + m
                return count

            seen[cc] = lax.fori_loop(0, 2 * blocks_k, body, seen[cc])

    kc = orbitals // 4

    far = jnp.where(hi < hi_n // 2, hi_n - 1, 0)
    near = jnp.where(hi < hi_n // 2, 0, 1)

    def o_copy(q, h, j, dest, sender):
        return pltpu.make_async_remote_copy(
            src_ref=res.at[q, j, pl.ds(pl.multiple_of(h * rows, rows), rows)],
            dst_ref=out_ref.at[:, pl.ds(pl.multiple_of(sender * width + j * w, BLOCK), w)],
            send_sem=o_send.at[q, h, j],
            recv_sem=o_recv.at[sender, j],
            device_id=(dest, c),
            device_id_type=MESH,
        )

    def o_local(h, j):
        return pltpu.make_async_copy(
            res.at[0, j, pl.ds(pl.multiple_of(h * rows, rows), rows)],
            out_ref.at[:, pl.ds(pl.multiple_of(r * width + j * w, BLOCK), w)],
            o_send.at[0, h, j],
        )

    def unit(q, j, start, count):
        g = (lo + q) % lo_n
        at = pl.ds(pl.multiple_of(start * rows, rows), count * rows)
        part = pl.ds(0, count * rows)
        acc[part] = jnp.zeros((count * rows, w), jnp.float32)

        def body(k, _):
            ks = pl.ds(pl.multiple_of(k * kc, kc), kc)
            acc[part] += jnp.dot(
                a_m[g, at, ks], b_m[j, ks, :], preferred_element_type=jnp.float32
            )
            return 0

        lax.fori_loop(0, orbitals // kc, body, 0)
        res[q, j, at] = acc[part].astype(jnp.bfloat16)
        for i in range(count):
            h = start + i
            dest = row_of(h, g)

            def wait_send(h=h, dest=dest):
                o_copy(q, h, j, dest, r).wait_send()

            def wait_local(h=h):
                o_local(h, j).wait()

            if q == 0:
                pl.when(hi != h)(lambda: o_copy(q, h, j, dest, r).start())
                pl.when(hi == h)(lambda: o_local(h, j).start())
                late.append((hi != h, wait_send))
                late.append((hi == h, wait_local))
            else:
                o_copy(q, h, j, dest, r).start()
                late.append((True, wait_send))

    def b_arrive(j):
        for e in range(1, x_n):
            for sign in (-1, 1):
                xx = x + sign * e
                there = jnp.logical_and(xx >= 0, xx < x_n)
                cc = xx * CORES + core
                pl.when(there)(lambda: b_wait(j, cc))
                onward = x - sign
                more = jnp.logical_and(there, jnp.logical_and(onward >= 0, onward < x_n))
                b_go(more, 0 if sign > 0 else 1, j, cc, onward * CORES + core)
                b_go(there, 2, j, cc, other)

    per_chunk = 2 * blocks_k * (w // BLOCK)
    needs = [-(-min(b_room, (j + 1) * per_chunk) // piece) for j in range(chunks)]

    def b_move(p, q):
        cc = (c + q) % n_col
        return pltpu.make_async_copy(
            b_raw.at[cc, b_part(p)], b_stage.at[cc, b_part(p)], staged.at[q])

    def b_finish(p):
        for xx in range(x_n):
            b_wait(p, xx * CORES + (core + 1) % CORES)
        if stage:
            for q in range(1, n_col):
                b_move(p, q).start()
            for q in range(1, n_col):
                b_move(p, q).wait()
            if p == 0:
                for own in own_b:
                    own.wait()
        else:
            own_b[p].wait()
        for j in range(chunks):
            if needs[j] == p + 1:
                mask_b(j)

    def line_arrive(d):
        for sign in (-1, 1):
            h = hi + sign * d
            there = jnp.logical_and(h >= 0, h < hi_n)
            pl.when(there)(lambda: a_wait(h, lo))
            onward = hi - sign
            more = jnp.logical_and(there, jnp.logical_and(onward >= 0, onward < hi_n))
            a_go(more, 0 if sign > 0 else 1, h, lo, row_of(onward, lo))
            a_lo_go(there, h)

    def at_distance(d):
        if d == 0:
            return [(hi, true)]
        out = []
        for sign in (-1, 1):
            h = hi + sign * d
            inside = jnp.logical_and(h >= 0, h < hi_n)
            out.append((h, jnp.logical_and(inside, h != far)))
        return out

    def lo_arrive(found):
        for h, there in found:
            for e in range(1, lo_n):
                for sign in (-1, 1):
                    l = lo + sign * e
                    ok = jnp.logical_and(there, jnp.logical_and(l >= 0, l < lo_n))
                    pl.when(ok)(lambda: a_wait(h, l))
                    onward = lo - sign
                    more = jnp.logical_and(ok, jnp.logical_and(onward >= 0, onward < lo_n))
                    a_go(more, 2 if sign > 0 else 3, h, l, row_of(hi, onward))
        for h, there in found:
            for q in range(1, lo_n):
                g = (lo + q) % lo_n
                pl.when(there)(lambda: mask_a(h, g))

    own_a.wait()
    mask_a(hi, lo)
    for d in range(1, hi_n):
        line_arrive(d)
        b_arrive(d - 1)
        for h, there in at_distance(d):
            pl.when(there)(lambda: mask_a(h, lo))
        lo_arrive(at_distance(d - 1))
        b_finish(d - 1)
    mask_a(far, lo)
    for p in range(hi_n - 1, chunks):
        b_arrive(p)
        b_finish(p)
    for j in range(chunks):
        unit(0, j, 0, hi_n)
    for j in range(chunks):
        for q in range(1, lo_n):
            unit(q, j, near, hi_n - 1)
    lo_arrive([(far, true)])
    for j in range(chunks):
        for q in range(1, lo_n):
            unit(q, j, far, 1)

    for q in range(1, n_row):
        sender = (r + q) % n_row
        for j in range(chunks):
            o_copy(0, 0, j, r, sender).wait_recv()
    for cond, wait in late:
        when_static(cond, wait)


def pack_kernel(dims, room, dense, t_ref, d_ref, tm_ref, dm_ref, pr_ref, pa_ref, pb_ref):
    n_row, n_col, _, _, _, chunks = dims
    a_room, b_room = room
    r = lax.axis_index("row")
    c = lax.axis_index("col")
    rows, orbitals = t_ref.shape
    _, piece_rows, width = d_ref.shape
    half, w = orbitals // 2, width // chunks
    blocks_k = piece_rows // BLOCK
    mask_row = (pr_ref[r * n_col + c] * rows) // BLOCK

    def a_body(jb, count):
        m = jnp.int32(1) if dense else tm_ref[mask_row, jb]

        @pl.when(jnp.logical_and(m > 0, count < a_room))
        def _():
            pa_ref[count] = t_ref[:, pl.ds(pl.multiple_of(jb * BLOCK, BLOCK), BLOCK)]

        return count + m

    a_count = lax.fori_loop(0, orbitals // BLOCK, a_body, jnp.int32(0))

    def a_clear(p, _):
        pa_ref[p] = jnp.zeros((rows, BLOCK), pa_ref.dtype)
        return 0

    lax.fori_loop(a_count, a_room, a_clear, 0)

    def b_body(i, count):
        kb, jh = i % blocks_k, i // blocks_k
        h, j = jh % 2, jh // 2
        k = h * half + c * piece_rows + kb * BLOCK
        for jb in range(w // BLOCK):
            m = jnp.int32(1) if dense else dm_ref[k // BLOCK, (r * width + j * w) // BLOCK + jb]

            @pl.when(jnp.logical_and(m > 0, count < b_room))
            def _():
                cols = pl.ds(pl.multiple_of(j * w + jb * BLOCK, BLOCK), BLOCK)
                pb_ref[count] = d_ref[h, pl.ds(pl.multiple_of(kb * BLOCK, BLOCK), BLOCK), cols]

            count = count + m
        return count

    b_count = lax.fori_loop(0, chunks * 2 * blocks_k, b_body, jnp.int32(0))

    def b_clear(p, _):
        pb_ref[p] = jnp.zeros((BLOCK, BLOCK), pb_ref.dtype)
        return 0

    lax.fori_loop(b_count, b_room, b_clear, 0)


def contract(dims, room, dense, number, tensor, density, tensor_mask, density_mask, pair_rows):
    n_row, n_col, hi_n, lo_n, x_n, chunks = dims
    a_room, b_room = room
    rows, orbitals = tensor.shape
    _, piece_rows, width = density.shape
    w = width // chunks
    bf16 = jnp.bfloat16
    any_spec = pl.BlockSpec(memory_space=pl.ANY)
    smem = pl.BlockSpec(memory_space=pltpu.SMEM)
    vmem = pl.BlockSpec(memory_space=pltpu.VMEM)
    packed = pl.pallas_call(
        functools.partial(pack_kernel, dims, room, dense),
        out_shape=[
            jax.ShapeDtypeStruct((a_room, rows, BLOCK), bf16),
            jax.ShapeDtypeStruct((b_room, BLOCK, BLOCK), bf16),
        ],
        in_specs=[vmem, vmem, smem, smem, smem],
        out_specs=[vmem, vmem],
        compiler_params=pltpu.CompilerParams(vmem_limit_bytes=60 << 20),
    )(tensor, density, tensor_mask, density_mask, pair_rows)
    return pl.pallas_call(
        functools.partial(kernel, dims, room),
        out_shape=jax.ShapeDtypeStruct((rows, orbitals), bf16),
        in_specs=[any_spec, any_spec, smem, smem, smem],
        out_specs=any_spec,
        scratch_shapes=[
            pltpu.VMEM((n_row, a_room, rows, BLOCK), bf16),
            pltpu.VMEM((lo_n, hi_n * rows, orbitals), bf16),
            pltpu.VMEM((n_col, b_room, BLOCK, BLOCK), bf16),
            pltpu.VMEM((chunks, orbitals, w), bf16),
            pltpu.VMEM((hi_n * rows, w), jnp.float32),
            pltpu.VMEM((lo_n, chunks, hi_n * rows, w), bf16),
            pltpu.SemaphoreType.DMA((n_row,)),
            pltpu.SemaphoreType.DMA((4, n_row)),
            pltpu.SemaphoreType.DMA((n_col, chunks)),
            pltpu.SemaphoreType.DMA((3, n_col, chunks)),
            pltpu.SemaphoreType.DMA((n_row, chunks)),
            pltpu.SemaphoreType.DMA((lo_n, hi_n, chunks)),
            pltpu.SemaphoreType.DMA((chunks + 1,)),
        ] + ([] if dense else [
            pltpu.VMEM((a_room, rows, BLOCK), bf16),
            pltpu.VMEM((n_col, b_room, BLOCK, BLOCK), bf16),
            pltpu.SemaphoreType.DMA((n_col + 1,)),
        ]),
        compiler_params=pltpu.CompilerParams(
            collective_id=number, has_side_effects=True, vmem_limit_bytes=60 << 20
        ),
    )(*packed, tensor_mask, density_mask, pair_rows)


def on_device(dims, *args):
    n_row, n_col, _, _, _, chunks = dims
    tensor, density, tensor_mask, density_mask, _ = args
    nb = tensor.shape[1] // BLOCK
    a_full = nb
    b_full = density.size // (BLOCK * BLOCK)

    def roomy(full, step):
        wanted = full // 2 + 2 * math.isqrt(full)
        return min(full, -(-wanted // step) * step)

    small = (roomy(a_full, 1), roomy(b_full, chunks))
    a_most = jnp.max(jnp.sum(tensor_mask, axis=1))
    b_most = jnp.max(jnp.sum(
        density_mask.reshape(2, n_col, nb // 2 // n_col, n_row, nb // n_row), axis=(0, 2, 4)))
    fits = jnp.logical_and(a_most <= small[0], b_most <= small[1])
    return lax.cond(
        fits,
        functools.partial(contract, dims, small, False, 0),
        functools.partial(contract, dims, (a_full, b_full), True, 1),
        *args,
    )


def solution(mesh):
    n_row, n_col = mesh.shape["row"], mesh.shape["col"]
    hi_n = 1
    while hi_n * hi_n < n_row:
        hi_n *= 2
    dims = (n_row, n_col, hi_n, n_row // hi_n, n_col // CORES, max(4, hi_n))
    placed = (P(("row", "col"), None), P(None, "col", "row"), P(), P(), P())
    return jax.shard_map(
        functools.partial(on_device, dims),
        mesh=mesh,
        in_specs=placed,
        out_specs=P(("row", "col"), None),
        check_vma=False,
    )
```

time: 128 us -> 121 us (0.945)
  Pallas kernels: 126 us -> 116 us
  other arithmetic: 0 us -> 2.25 us
  between operations: 0.01 us -> 1.33 us
    pallas_call x1 -> x2, Pallas kernels: 126 us -> 116 us  [the longest x1 106 us: contract(): pl.pallas_call(functools.partial(kernel, dims, room), out_shape=jax.Shape...]
    unnamed x1, local copies, waits for them, and re-layouts: 2.26 us -> 0.97 us
where the time goes in v2:
time: 121 us
  Pallas kernels  116 us (96%)
  other arithmetic  2.25 us (2%)
  local copies, waits for them, and re-layouts  1.87 us (2%)
  between operations  1.33 us (1%)
    pallas_call x1, Pallas kernels, contract(): pl.pallas_call(functools.partial(kernel, dims, room), out_shape=jax.Shape...  106 us
    pallas_call x1, Pallas kernels, contract(): pl.pallas_call(functools.partial(pack_kernel, dims, room, dense), out_sha...  9.49 us

profile of v2, /device:TPU:0, one launch (start us, length us, event | category | flops | bytes accessed | tf_op | source)
XLA Modules:
  0.0 121.1 jit_solution(4614315728367807442)
XLA Ops:
  0.0 0.8 reduce_sum.18
  0.8 0.6 reduce_max.18
  2.1 0.9 reshape.3
  3.0 0.2 reduce_sum.19
  3.2 0.6 reduce_max.19
  4.5 115.7 %conditional.1 = (bf16[64,8192]{1,0:T(8,128)(2,1)S(1)}) conditional(s32[]{:T(128)} %convert_element_type.3, (bf16[64,8192]{1,0:T(8,128)(2,1)}, bf16[2,1024,1024]{2,1,0:T(8,128)(2,1)}, s32[16,64]{1,0:T(8,128)}, s32[64,64]{1,0:T(8,128)}, s32[32]{0:T(128)}) %tuple.11, (bf16[64,8192]{1,0:T(8,128)(2,1)}, bf16[2,1024,1024]{2,1,0:T(8,128)(2,1)}, ...), branch_computations={%region_4.0_spmd, %region_5.0_spmd} | conditional | bytes 82524 | solution.py:453
  4.5 0.0 copy-start.1
  4.5 0.0 copy-start.3
  4.5 0.0 copy-start.5
  4.5 9.5 %branch_1_fun.2 = (bf16[48,64,128]{2,1,0:T(8,128)(2,1)}, bf16[88,128,128]{2,1,0:T(8,128)(2,1)}) custom-call(bf16[64,8192]{1,0:T(8,128)(2,1)} %get-tuple-element.50.t_ref, bf16[2,1024,1024]{2,1,0:T(8,128)(2,1)} %get-tuple-element.52.d_ref, s32[16,64]{1,0:T(8,128)} %get-tuple-element.37.tm_ref, s32[64,64]{1,0:T(8,128)} %get-tuple-element.38.dm_ref, ...), custom_call_target="tpu_custom_call" | custom-call | tf_op jit(solution)/shard_map/cond/branch_1_fun/pallas_call | solution.py:397
  14.0 0.0 copy-done.1
  14.0 0.0 copy-done.3
  14.0 0.0 copy-done.5
  14.0 106.1 %branch_1_fun.3 = bf16[64,8192]{1,0:T(8,128)(2,1)S(1)} custom-call(bf16[48,64,128]{2,1,0:T(8,128)(2,1)} %get-tuple-element.40.pa_ref, bf16[88,128,128]{2,1,0:T(8,128)(2,1)} %get-tuple-element.41.pb_ref, s32[16,64]{1,0:T(8,128)S(1)} %copy-done.3, s32[64,64]{1,0:T(8,128)S(1)} %copy-done.1, s32[32]{0:T(128)S(1)} %copy-done.5), custom_call_target="tpu_custom_call" | custom-call | tf_op jit(solution)/shard_map/cond/branch_1_fun/pallas_call | solution.py:407
  120.1 1.0 copy.17
Async XLA Ops:
  4.5 9.5 %copy-start.1 = (s32[64,64]{1,0:T(8,128)S(1)}, s32[64,64]{1,0:T(8,128)}, u32[]{:S(2)}) copy-start(s32[64,64]{1,0:T(8,128)} %get-tuple-element.38.dm_ref) | copy-start | bytes 49156 | tf_op jit(solution)/shard_map/cond
  4.5 9.5 %copy-start.3 = (s32[16,64]{1,0:T(8,128)S(1)}, s32[16,64]{1,0:T(8,128)}, u32[]{:S(2)}) copy-start(s32[16,64]{1,0:T(8,128)} %get-tuple-element.37.tm_ref) | copy-start | bytes 12292 | tf_op jit(solution)/shard_map/cond
  4.5 9.5 %copy-start.5 = (s32[32]{0:T(128)S(1)}, s32[32]{0:T(128)}, u32[]{:S(2)}) copy-start(s32[32]{0:T(128)} %get-tuple-element.54.pr_ref) | copy-start | bytes 388 | tf_op jit(solution)/shard_map/cond

commit v3 on v2

--- a/solution.py
+++ b/solution.py
@@ -441,11 +441,11 @@
     a_full = nb
     b_full = density.size // (BLOCK * BLOCK)
 
-    def roomy(full, step):
-        wanted = full // 2 + 2 * math.isqrt(full)
+    def roomy(full, step, margin):
+        wanted = full // 2 + margin * math.isqrt(full) // 2
         return min(full, -(-wanted // step) * step)
 
-    small = (roomy(a_full, 1), roomy(b_full, chunks))
+    small = (roomy(a_full, 1, 3), roomy(b_full, chunks, 4))
     a_most = jnp.max(jnp.sum(tensor_mask, axis=1))
     b_most = jnp.max(jnp.sum(
         density_mask.reshape(2, n_col, nb // 2 // n_col, n_row, nb // n_row), axis=(0, 2, 4)))

time: 121 us -> 120 us (level)
  Pallas kernels: 116 us -> 114 us
    pallas_call x1, Pallas kernels: 106 us -> 105 us  [contract(): pl.pallas_call(functools.partial(kernel, dims, room), out_shape=jax.Shape...]
where the time goes in v3:
time: 120 us
  Pallas kernels  114 us (95%)
  other arithmetic  2.25 us (2%)
  local copies, waits for them, and re-layouts  1.87 us (2%)
  between operations  1.33 us (1%)
    pallas_call x1, Pallas kernels, contract(): pl.pallas_call(functools.partial(kernel, dims, room), out_shape=jax.Shape...  105 us
    pallas_call x1, Pallas kernels, contract(): pl.pallas_call(functools.partial(pack_kernel, dims, room, dense), out_sha...  9.5 us

profile of v3, /device:TPU:0, one launch (start us, length us, event | category | flops | bytes accessed | tf_op | source)
XLA Modules:
  0.0 119.9 jit_solution(2016183917570309077)
XLA Ops:
  0.0 0.8 reduce_sum.18
  0.8 0.6 reduce_max.18
  2.1 0.9 reshape.3
  3.0 0.2 reduce_sum.19
  3.2 0.6 reduce_max.19
  4.5 114.4 %conditional.1 = (bf16[64,8192]{1,0:T(8,128)(2,1)S(1)}) conditional(s32[]{:T(128)} %convert_element_type.3, (bf16[64,8192]{1,0:T(8,128)(2,1)}, bf16[2,1024,1024]{2,1,0:T(8,128)(2,1)}, s32[16,64]{1,0:T(8,128)}, s32[64,64]{1,0:T(8,128)}, s32[32]{0:T(128)}) %tuple.11, (bf16[64,8192]{1,0:T(8,128)(2,1)}, bf16[2,1024,1024]{2,1,0:T(8,128)(2,1)}, ...), branch_computations={%region_4.0_spmd, %region_5.0_spmd} | conditional | bytes 82524 | solution.py:453
  4.5 0.0 copy-start.1
  4.5 0.0 copy-start.3
  4.5 0.0 copy-start.5
  4.5 9.5 %branch_1_fun.2 = (bf16[44,64,128]{2,1,0:T(8,128)(2,1)}, bf16[88,128,128]{2,1,0:T(8,128)(2,1)}) custom-call(bf16[64,8192]{1,0:T(8,128)(2,1)} %get-tuple-element.50.t_ref, bf16[2,1024,1024]{2,1,0:T(8,128)(2,1)} %get-tuple-element.52.d_ref, s32[16,64]{1,0:T(8,128)} %get-tuple-element.37.tm_ref, s32[64,64]{1,0:T(8,128)} %get-tuple-element.38.dm_ref, ...), custom_call_target="tpu_custom_call" | custom-call | tf_op jit(solution)/shard_map/cond/branch_1_fun/pallas_call | solution.py:397
  14.0 0.0 copy-done.1
  14.0 0.0 copy-done.3
  14.0 0.0 copy-done.5
  14.0 104.9 %branch_1_fun.3 = bf16[64,8192]{1,0:T(8,128)(2,1)S(1)} custom-call(bf16[44,64,128]{2,1,0:T(8,128)(2,1)} %get-tuple-element.40.pa_ref, bf16[88,128,128]{2,1,0:T(8,128)(2,1)} %get-tuple-element.41.pb_ref, s32[16,64]{1,0:T(8,128)S(1)} %copy-done.3, s32[64,64]{1,0:T(8,128)S(1)} %copy-done.1, s32[32]{0:T(128)S(1)} %copy-done.5), custom_call_target="tpu_custom_call" | custom-call | tf_op jit(solution)/shard_map/cond/branch_1_fun/pallas_call | solution.py:407
  118.9 1.0 copy.17
Async XLA Ops:
  4.5 9.5 %copy-start.1 = (s32[64,64]{1,0:T(8,128)S(1)}, s32[64,64]{1,0:T(8,128)}, u32[]{:S(2)}) copy-start(s32[64,64]{1,0:T(8,128)} %get-tuple-element.38.dm_ref) | copy-start | bytes 49156 | tf_op jit(solution)/shard_map/cond
  4.5 9.5 %copy-start.3 = (s32[16,64]{1,0:T(8,128)S(1)}, s32[16,64]{1,0:T(8,128)}, u32[]{:S(2)}) copy-start(s32[16,64]{1,0:T(8,128)} %get-tuple-element.37.tm_ref) | copy-start | bytes 12292 | tf_op jit(solution)/shard_map/cond
  4.5 9.5 %copy-start.5 = (s32[32]{0:T(128)S(1)}, s32[32]{0:T(128)}, u32[]{:S(2)}) copy-start(s32[32]{0:T(128)} %get-tuple-element.54.pr_ref) | copy-start | bytes 388 | tf_op jit(solution)/shard_map/cond
